TPU v7x, 32 devices: a whole 2x2x4 slice. The times are simulated.
32 devices in a mesh: sec: 4 (over y, core), dev: 8 (over z, x).
Axes of the slice: x: 2, y: 2, z: 4, core: 2. Of those that a mesh axis runs over, the one named last changes fastest.
Arguments:
- potential: float32 [64, 32, 512], P('dev', None, 'sec'), may hold values from -6 to 6
- previous: float32 [64, 32, 512], P('dev', None, 'sec'), may hold values from -6 to 6
- wave_coeff: float32 [64, 32, 512], P('dev', None, 'sec'), may hold values from 0.03 to 0.16
- sketch_in: bfloat16 [16384, 512], P('dev'), may hold values from -6 to 6
- omega: float32 [64, 512], replicated, may hold values from -6 to 6
- blocks: int32 [8, 9], P('dev'), may hold values from 0 to 255, as said below
- owners: int32 [8, 9], P('dev'), may hold values from 0 to 7, as said below
Outputs:
- basis: bfloat16 [4, 16384, 512], P('sec', 'dev')
- gram_factor: float32 [4, 512, 512], P('sec')
Inputs may be any that keep to these rules, and one draw needn't show every extreme that they name: `blocks`: within one section's 3 entries of a row the block numbers are distinct. Within a row of owners no owner appears more than 2 times, and one owner, the same for all rows, appears exactly 2 times in every row.
All inputs are finite; a program needn't handle non-finite values.
Results may differ from a plain program's by a relative error of at most 0.003.
Values sent between devices are 32-bit elements; how exact they have to be, the bound alone decides.
No kernel may reach another device: no remote copies, remote signals or barrier semaphores. Data moves between devices by JAX's collectives and lax.ppermute only.
A program may use at most 256 MiB of HBM per device.

v0:
```python
import functools
import math

import jax
import jax.numpy as jnp
import numpy as np
from jax import lax
from jax.experimental import pallas as pl
from jax.experimental.pallas import tpu as pltpu
from jax.sharding import PartitionSpec as P

CAP = 2
damping = 0.05
LANES = 128
highest = lax.Precision.HIGHEST
decay = math.sqrt(1.0 - damping)
BOTH = ("sec", "dev")


def neighbour_path(columns):
    order = []
    for i in range(0, columns, 2):
        pair = [i, i + 1]
        order += pair if (i // 2) % 2 == 0 else pair[::-1]
    return order


def vmem(*arrays):
    return [pl.BlockSpec(memory_space=pltpu.VMEM)] * len(arrays)


def big(limit=48):
    return pltpu.CompilerParams(vmem_limit_bytes=limit << 20)


def slab_of(order, column, section, per_slab):
    place = order.index(column)
    forward, backward = place // per_slab, (len(order) - 1 - place) // per_slab
    return jnp.where(section % 2 == 0, forward, backward)


def split_kernel(order, slab, per_slab, u_ref, e_ref, k_ref, blocks_ref, owners_ref, out_ref, turned):
    section = lax.axis_index("sec")
    extent_x, extent_y, depth = u_ref.shape
    for a, ref in enumerate((u_ref, e_ref, k_ref)):
        for p in range(2):
            rows = jnp.concatenate([ref[x] for x in range(p, extent_x, 2)], axis=0)
            if a == 1:
                rows = rows * decay
            turned[2 * a + p] = rows.T
    for column in range(len(order)):
        at = slab_of(order, column, section, per_slab)
        start = pl.multiple_of(at * slab, 8)
        for q in range(6):
            out_ref[column, q * slab : (q + 1) * slab, :] = turned[q, pl.ds(start, slab), :]
        for r, ref in enumerate((blocks_ref, owners_ref)):
            out_ref[column, 6 * slab + r : 6 * slab + r + 1, : ref.shape[1]] = ref[...].astype(
                jnp.float32
            )


def steps_kernel(*args):
    last, sections = args[3], args[5]
    if last:
        flag_ref = args[16]
        flag_ref[0] = 0

    @pl.when(lax.axis_index("sec") < sections - 1)
    def _():
        evolve(*args)


def evolve(
    first_step, slab, per_device, last, snaps, sections,
    table, kl, kc, kr, sl, sc, sr, w_in, *rest,
):
    if last:
        send_ref, over_ref, flag_ref, w_ref, field_a, field_b, gain, own, used = rest
    else:
        state_ref, w_ref, field_a, field_b, gain, own = rest
    list_start = lax.axis_index("sec") * per_device
    columns = kc.shape[0]
    rows = 3 * slab
    lane = lax.broadcasted_iota(jnp.int32, (8, LANES), 1)
    y_first, y_last = lane % 32 == 0, lane % 32 == 31
    zero = jnp.zeros((8, LANES), jnp.float32)

    for o in range(2 * columns):
        d, p = o // 2, o % 2
        for field, at in ((field_a, p), (field_b, 2 + p)):
            field[o, 0:8, :] = zero
            field[o, 8 + rows : 16 + rows, :] = zero
            for h, ref in enumerate((sl, sc, sr)):
                field[o, 8 + h * slab : 8 + (h + 1) * slab, :] = ref[
                    d, at * slab : (at + 1) * slab, :
                ]
        for h, ref in enumerate((kl, kc, kr)):
            k = ref[d, (4 + p) * slab : (5 + p) * slab, :]
            gain[o, h * slab : (h + 1) * slab, :] = k * (1.0 / decay)
            own[o, h * slab : (h + 1) * slab, :] = ((2.0 - damping) - 6.0 * k) * (1.0 / decay)
    w_ref[...] = w_in[...]

    def step(src, dst, tiles, number):
        for z in tiles:
            at = slice(8 + 8 * z, 16 + 8 * z)
            low = slice(7 + 8 * z, 15 + 8 * z)
            high = slice(9 + 8 * z, 17 + 8 * z)
            here = slice(8 * z, 8 * z + 8)
            values = [src[o, at, :] for o in range(2 * columns)]
            up = [pltpu.roll(values[2 * d + 1], 32, 1) for d in range(columns)]
            down = [pltpu.roll(values[2 * d], LANES - 32, 1) for d in range(columns)]
            for o in range(2 * columns):
                d, p = o // 2, o % 2
                v = values[o]
                if p == 0:
                    side = jnp.where(lane < 32, up[d - 1] if d > 0 else zero, up[d])
                    total = values[o + 1] + side
                else:
                    side = jnp.where(
                        lane >= LANES - 32, down[d + 1] if d + 1 < columns else zero, down[d]
                    )
                    total = values[o - 1] + side
                total = total + (src[o, low, :] + src[o, high, :])
                total = total + jnp.where(y_first, 0.0, pltpu.roll(v, 1, 1))
                total = total + jnp.where(y_last, 0.0, pltpu.roll(v, LANES - 1, 1))
                dst[o, at, :] = own[o, here, :] * v + gain[o, here, :] * total - dst[o, at, :]

        def column_blocks(d, carry):
            for i in range(per_device):
                block = table[d, 0, list_start + i]
                x, y = block >> 5, block & 31
                at_lane = ((x >> 1) << 5) + y
                o = 2 * d + (x & 1)
                j = d * per_device + i
                held = w_ref[j]
                for h in range(slab // 8):
                    target = h * snaps + number
                    value = dst[o, 8 + slab + 8 * h : 16 + slab + 8 * h, :]
                    moved = pltpu.roll(value, (target - at_lane) & (LANES - 1), 1)
                    held = jnp.where(lane == target, moved, held)
                w_ref[j] = held
            return carry

        lax.fori_loop(0, columns, column_blocks, 0, unroll=min(columns, 8))

    for phase in range(slab // 8):
        tiles = range(phase, 3 * slab // 8 - phase)

        def pair(m, carry):
            number = first_step + 8 * phase + 2 * m
            step(field_a, field_b, tiles, number)
            step(field_b, field_a, tiles, number + 1)
            return carry

        lax.fori_loop(0, 4, pair, 0)

    if last:
        half = send_ref.shape[1]
        for d in range(columns):
            used[d] = 0

        def place(d, carry):
            for i in range(per_device):
                mine = table[d, 1, list_start + i]
                n = used[mine]
                used[mine] = n + 1

                @pl.when(n < half)
                def _(i=i, mine=mine, n=n):
                    send_ref[mine, n] = w_ref[d * per_device + i]

                @pl.when(n >= half)
                def _(i=i, mine=mine, n=n):
                    over_ref[mine, n - half] = w_ref[d * per_device + i]

            return carry

        lax.fori_loop(0, columns, place, 0)
        for d in range(columns):
            flag_ref[0] = jnp.maximum(flag_ref[0], jnp.where(used[d] > half, 1, 0))
    else:
        for o in range(2 * columns):
            d, p = o // 2, o % 2
            state_ref[d, p * slab : (p + 1) * slab, :] = field_a[o, 8 + slab : 8 + 2 * slab, :]
            state_ref[d, (2 + p) * slab : (3 + p) * slab, :] = field_b[
                o, 8 + slab : 8 + 2 * slab, :
            ]


def unpack(tile, h, snaps, lane):
    if h:
        tile = pltpu.roll(tile, LANES - h * snaps, 1)
    return jnp.where(lane < snaps, tile, 0.0)


def product_kernel(*args):
    sections = args[4]

    @pl.when(lax.axis_index("sec") < sections - 1)
    def _():
        products(*args)


def products(
    order, slab, per_slab, snaps, sections, table, w_ref, over_ref, s_ref, out_ref, wide
):
    section = lax.axis_index("sec")
    me = lax.axis_index("dev")
    columns = len(order)
    per_device = table.shape[2] // (sections - 1)
    list_start = section * per_device
    half = w_ref.shape[1]
    lane = lax.broadcasted_iota(jnp.int32, (8, LANES), 1)
    wide[...] = jnp.zeros(wide.shape, jnp.float32)

    def place(ref, n, slot):
        for column in range(columns):
            if order.index(column) % per_slab:
                continue
            at = slab_of(order, column, section, per_slab)
            tile = ref[column, n]
            for h in range(slab // 8):
                w = unpack(tile, h, snaps, lane)
                w1 = w.astype(jnp.bfloat16).astype(jnp.float32)
                w2 = (w - w1).astype(jnp.bfloat16).astype(jnp.float32)
                start = pl.multiple_of(slot * LANES + at * slab + 8 * h, 8)
                wide[pl.ds(start, 8), :] = w1 + pltpu.roll(w2, snaps, 1)

    def row(d, n):
        def earlier(m, c):
            return c + jnp.where(table[d, 1, m] == me, 1, 0)

        count = lax.fori_loop(0, list_start, earlier, 0)
        for i in range(per_device):
            mine = table[d, 1, list_start + i] == me
            slot = d * CAP + count

            @pl.when(jnp.logical_and(mine, n < half))
            def _(n=n, slot=slot):
                place(w_ref, n, slot)

            @pl.when(jnp.logical_and(mine, n >= half))
            def _(n=n, slot=slot):
                place(over_ref, n - half, slot)

            step = jnp.where(mine, 1, 0)
            n, count = n + step, count + step
        return n

    lax.fori_loop(0, columns, row, 0)
    both = wide[...].astype(jnp.bfloat16)
    dot = functools.partial(
        lax.dot_general,
        dimension_numbers=(((0,), (0,)), ((), ())),
        preferred_element_type=jnp.float32,
    )
    cross = dot(both, s_ref[...])
    cross = cross[:snaps] + cross[snaps:]
    inner = dot(both, both)
    inner = inner[:snaps, :] + inner[snaps:, :]
    inner = inner + pltpu.roll(inner, snaps, 1)
    strips = cross.shape[1] // LANES
    share = out_ref.shape[1]
    for r in range(snaps // 8):
        here = slice(8 * r, 8 * r + 8)
        for c in range(strips):
            at = r * (strips + 1) + c
            out_ref[at // share, at % share] = cross[here, c * LANES : (c + 1) * LANES]
        at = r * (strips + 1) + strips
        out_ref[at // share, at % share] = inner[here, :]


def three(x):
    x1 = x.astype(jnp.bfloat16)
    rest = x - x1.astype(jnp.float32)
    x2 = rest.astype(jnp.bfloat16)
    return x1, x2, (rest - x2.astype(jnp.float32)).astype(jnp.bfloat16)


def reciprocal(x):
    guess = pl.reciprocal(x, approx=True)
    return guess * (2.0 - x * guess)


def factor_block(d, e, sub, lane, spread):
    tiles = len(d)

    def wide(x):
        return jnp.broadcast_to(x, (8, LANES))

    def stack(values):
        out = values[0]
        for j in range(1, 8):
            out = jnp.where(sub == j, values[j], out)
        return out

    for p in range(tiles):
        first = 8 * p
        cols = [wide(d[p][:, first + j : first + j + 1]) for j in range(8)]
        base = 80 * (p % 2)
        for k, value in enumerate(cols + [d[p], e[p]]):
            spread[base + 8 * k : base + 8 * k + 8, :] = value

        def row(k, j, base=base):
            return spread[pl.ds(base + 8 * k + j, 8, stride=0), :]

        s = [[row(k, j) if k >= j else None for k in range(8)] for j in range(8)]
        t = [row(8, j) for j in range(8)]
        te = [row(9, j) for j in range(8)]
        inv, m = [], [[None] * 8 for _ in range(8)]
        for j in range(0, 8, 2):
            n = j + 1
            a, b, c = s[j][j], s[j][n], s[n][n]
            det = a * c - b * b
            inv_a, inv_det = reciprocal(a), reciprocal(det)
            inv += [inv_a, a * inv_det]
            m[j][n] = b * inv_a
            s[n][n] = det * inv_a
            t[n] = t[n] - m[j][n] * t[j]
            te[n] = te[n] - m[j][n] * te[j]
            for k in range(j + 2, 8):
                m[j][k] = s[j][k] * inv_a
                m[n][k] = (a * s[n][k] - b * s[j][k]) * inv_det
                s[n][k] = s[n][k] - m[j][n] * s[j][k]
            for k in range(j + 2, 8):
                for i in range(k, 8):
                    s[k][i] = (s[k][i] - m[j][k] * s[j][i]) - m[n][k] * s[n][i]
                t[k] = (t[k] - m[j][k] * t[j]) - m[n][k] * t[n]
                te[k] = (te[k] - m[j][k] * te[j]) - m[n][k] * te[n]
        if p + 1 < tiles:
            z, ze = [None] * 8, [None] * 8
            for j in reversed(range(8)):
                z[j], ze[j] = t[j] * inv[j], te[j] * inv[j]
                for k in range(j + 1, 8):
                    z[j] = z[j] - m[j][k] * z[k]
                    ze[j] = ze[j] - m[j][k] * ze[k]
            i = p + 1
            parts, parts_e = [], []
            for j in range(8):
                col = wide(d[i][:, first + j : first + j + 1])
                parts.append(col * z[j])
                parts_e.append(col * ze[j])
            while len(parts) > 1:
                parts = [x + y for x, y in zip(parts[::2], parts[1::2])]
                parts_e = [x + y for x, y in zip(parts_e[::2], parts_e[1::2])]
            if p + 2 < tiles:
                p1, p2, p3 = three(d[p])
                z1, z2, z3 = three(jnp.concatenate([stack(z), stack(ze)], axis=1))
                change = lax.dot_general(
                    jnp.concatenate([p1, p1, p1, p2, p2, p3], axis=0),
                    jnp.concatenate([z1, z2, z3, z1, z2, z1], axis=0),
                    (((0,), (0,)), ((), ())),
                    preferred_element_type=jnp.float32,
                )
                for n in range(p + 2, tiles):
                    d[n] = d[n] - change[8 * n : 8 * n + 8, :LANES]
                    e[n] = e[n] - change[8 * n : 8 * n + 8, LANES:]
            d[i], e[i] = d[i] - parts[0], e[i] - parts_e[0]
        roots = [lax.rsqrt(s[j][j]) for j in range(8)]
        d[p] = jnp.where(lane >= sub + first, stack([t[j] * roots[j] for j in range(8)]), 0.0)
        e[p] = stack([te[j] * roots[j] for j in range(8)])
    return jnp.concatenate(d, axis=0), jnp.concatenate(e, axis=0)


def factor_kernel(scale, sections, *refs):
    factor_ref = refs[3]
    analysis = lax.axis_index("sec") == sections - 1

    @pl.when(analysis)
    def _():
        factorize(scale, *refs)

    @pl.when(jnp.logical_not(analysis))
    def _():
        factor_ref[...] = jnp.zeros(factor_ref.shape, jnp.float32)


def factorize(
    scale, parts_ref, omega_ref, s_ref, factor_ref, inverse_ref, g, inner_ref, spread
):
    rank = s_ref.shape[0]
    snaps = omega_ref.shape[0]
    strips = rank // LANES
    rows_first = (((0,), (0,)), ((), ()))

    def band(r, c):
        return parts_ref[r * (strips + 1) + c]

    cross = jnp.concatenate(
        [
            jnp.concatenate([band(r, c) for c in range(strips)], axis=1)
            for r in range(snaps // 8)
        ],
        axis=0,
    )
    inner = jnp.concatenate([band(r, strips) for r in range(snaps // 8)], axis=0)
    omega = omega_ref[...]
    half = cross + 0.5 * jnp.dot(
        inner[:, :snaps], omega, precision=highest, preferred_element_type=jnp.float32
    )
    left = jnp.concatenate([half, omega], axis=0)
    right = jnp.concatenate([omega, half], axis=0)
    g[...] = s_ref[...] + lax.dot_general(
        left, right, rows_first, precision=highest, preferred_element_type=jnp.float32
    )
    inverse_ref[...] = jnp.zeros(inverse_ref.shape, jnp.float32)
    inner_ref[...] = jnp.zeros(inner_ref.shape, jnp.float32)
    factor_ref[...] = jnp.zeros(factor_ref.shape, jnp.float32)
    sub = lax.broadcasted_iota(jnp.int32, (8, LANES), 0)
    lane = lax.broadcasted_iota(jnp.int32, (8, LANES), 1)
    tiles = LANES // 8

    def rows_of(k):
        return slice(k * LANES, (k + 1) * LANES)

    for k in range(strips):
        here = rows_of(k)
        d = [g[k * LANES + 8 * i : k * LANES + 8 * i + 8, here] for i in range(tiles)]
        e = [jnp.where(lane == sub + 8 * i, 1.0, 0.0) for i in range(tiles)]
        upper, small = factor_block(d, e, sub, lane, spread.at[k % 2])
        factor_ref[here, here] = upper * (1.0 / scale)
        small_rows = [small]
        if k + 1 < strips:
            right = slice((k + 1) * LANES, rank)
            fresh = jnp.dot(
                small, g[here, right], precision=highest, preferred_element_type=jnp.float32
            )
            factor_ref[here, right] = fresh * (1.0 / scale)
            change = functools.partial(
                lax.dot_general,
                dimension_numbers=rows_first,
                precision=highest,
                preferred_element_type=jnp.float32,
            )
            following = rows_of(k + 1)
            g[following, right] = g[following, right] - change(fresh[:, :LANES], fresh)
            if k + 2 < strips:
                later = slice((k + 2) * LANES, rank)
                g[later, later] = g[later, later] - change(fresh[:, LANES:], fresh[:, LANES:])
        if k:
            left = slice(0, k * LANES)
            small_rows = [
                jnp.dot(
                    small, inner_ref[here, left], precision=highest,
                    preferred_element_type=jnp.float32,
                ),
                small,
            ]
        done = jnp.concatenate(small_rows, axis=1)
        if k + 1 < strips:
            upto = slice(0, (k + 1) * LANES)
            inner_ref[right, upto] = inner_ref[right, upto] - change(fresh, done)
        inverse_ref[0 : (k + 1) * LANES, here] = (done * scale).T


def basis_kernel(sections, inverse_ref, omega_ref, s_ref, *rest):
    pieces, out_ref, stack = rest[:-2], rest[-2], rest[-1]
    analysis = lax.axis_index("sec") == sections - 1
    rank, snaps = inverse_ref.shape[0], omega_ref.shape[0]
    band = 2 * LANES
    dot = functools.partial(jnp.dot, preferred_element_type=jnp.float32)

    @pl.when(jnp.logical_and(analysis, pl.program_id(0) == 0))
    def _():
        def split(x):
            high = x.astype(jnp.bfloat16)
            return high, (x - high.astype(jnp.float32)).astype(jnp.bfloat16)

        inverse = inverse_ref[...]
        mixed = dot(omega_ref[...], inverse, precision=highest)
        x1, x2 = split(inverse)
        m1, m2 = split(jnp.concatenate([mixed, mixed], axis=0))
        for to in range(band, rank + 1, band):
            cols = slice(to - band, to)
            stack[: 2 * to + 4 * snaps, cols] = jnp.concatenate(
                [x1[:to, cols], x2[:to, cols], m1[:, cols], m2[:, cols]], axis=0
            )

    @pl.when(analysis)
    def _():
        s = s_ref[...]
        w = pieces[0][...]
        for piece in pieces[1:]:
            w = w + piece[...]
        w = w.astype(jnp.bfloat16)
        for to in range(band, rank + 1, band):
            left = jnp.concatenate([s[:, :to], s[:, :to], w, w], axis=1)
            q = dot(left, stack[: 2 * to + 4 * snaps, to - band : to])
            out_ref[:, to - band : to] = q.astype(jnp.bfloat16)

    @pl.when(jnp.logical_not(analysis))
    def _():
        out_ref[...] = jnp.zeros(out_ref.shape, jnp.bfloat16)


def shards(potential, previous, wave_coeff, sketch_in, omega, blocks, owners):
    sections = lax.axis_size("sec")
    columns = lax.axis_size("dev")
    devices = sections * columns
    extent_x, extent_y, depth = potential.shape
    list_width = owners.shape[1]
    per_device = list_width // (sections - 1)
    snaps, rank = omega.shape
    slab = max(8, depth // columns)
    per_slab = slab * columns // depth
    slots = columns * CAP
    order = neighbour_path(columns)
    path = []
    for section in range(sections - 1):
        path += [section * columns + d for d in (order if section % 2 == 0 else order[::-1])]
    up = [(path[i], path[i + per_slab]) for i in range(len(path) - per_slab)]
    down = [(b, a) for a, b in up]
    f32 = jnp.float32

    analysis = lax.axis_index("sec") == sections - 1

    def whole_gram():
        own = lax.dot_general(
            sketch_in, sketch_in, (((0,), (0,)), ((), ())), preferred_element_type=f32
        )
        own = own.reshape(columns, rank // columns, rank)
        own = lax.all_to_all(own, "dev", split_axis=0, concat_axis=0, tiled=True)
        own = jnp.broadcast_to(jnp.sum(own, axis=0)[None], own.shape)
        own = lax.all_to_all(own, "dev", split_axis=0, concat_axis=0, tiled=True)
        return own.reshape(rank, rank)

    scaled = omega * jnp.asarray(
        decay ** np.arange(1, snaps + 1, dtype=np.float64), f32
    )[:, None]

    chunk = 6 * slab + 8
    operands = (potential, previous, wave_coeff, blocks, owners)
    outgoing = pl.pallas_call(
        functools.partial(split_kernel, order, slab, per_slab),
        out_shape=jax.ShapeDtypeStruct((columns, chunk, LANES), f32),
        in_specs=vmem(*operands),
        out_specs=pl.BlockSpec(memory_space=pltpu.VMEM),
        scratch_shapes=[pltpu.VMEM((6, depth, LANES), f32)],
        compiler_params=big(),
    )(*operands)
    raw = lax.all_to_all(outgoing, "dev", split_axis=0, concat_axis=0, tiled=True)
    gram, scaled, raw = lax.optimization_barrier(
        (lax.cond(analysis, whole_gram, lambda: jnp.zeros((rank, rank), f32)), scaled, raw)
    )
    table = raw[:, 6 * slab : 6 * slab + 2, :list_width].astype(jnp.int32)

    def sides(x):
        return lax.ppermute(x, BOTH, up), x, lax.ppermute(x, BOTH, down)

    fields = sides(raw)
    state = fields
    held = jnp.zeros((columns * per_device, 8, LANES), f32)
    rounds = snaps // slab
    for number in range(rounds):
        last = number == rounds - 1
        operands = (table, *fields, *state, held)
        sent = jax.ShapeDtypeStruct((columns, slots // 2, 8, LANES), f32)
        flag = jax.ShapeDtypeStruct((1,), jnp.int32)
        result = [sent, sent, flag] if last else [jax.ShapeDtypeStruct((columns, 4 * slab, LANES), f32)]
        *moved, held = pl.pallas_call(
            functools.partial(
                steps_kernel, number * slab, slab, per_device, last, snaps, sections
            ),
            out_shape=(*result, jax.ShapeDtypeStruct(held.shape, f32)),
            in_specs=[pl.BlockSpec(memory_space=pltpu.SMEM)] + vmem(*operands[1:]),
            out_specs=tuple(
                pl.BlockSpec(memory_space=pltpu.SMEM if x.dtype == jnp.int32 else pltpu.VMEM)
                for x in (*result, held)
            ),
            scratch_shapes=[pltpu.VMEM((2 * columns, 3 * slab + 16, LANES), f32)] * 2
            + [pltpu.VMEM((2 * columns, 3 * slab, LANES), f32)] * 2
            + [pltpu.SMEM((columns,), jnp.int32)] * last,
            compiler_params=big(),
        )(*operands)
        if not last:
            state = sides(moved[0])

    def trade(x):
        return lax.all_to_all(x, "dev", split_axis=0, concat_axis=0, tiled=True)

    arrived = trade(moved[0])
    over = lax.cond(moved[2][0] > 0, trade, lambda x: x, moved[1])
    operands = (table, arrived, over, sketch_in)
    bands = (snaps // 8) * (rank // LANES + 1)
    share = -(-bands // columns)
    parts, wide = pl.pallas_call(
        functools.partial(product_kernel, order, slab, per_slab, snaps, sections),
        out_shape=(
            jax.ShapeDtypeStruct((columns, share, 8, LANES), f32),
            jax.ShapeDtypeStruct((slots * depth, LANES), f32),
        ),
        in_specs=[pl.BlockSpec(memory_space=pltpu.SMEM)] + vmem(*operands[1:]),
        out_specs=tuple(vmem(0, 0)),
        compiler_params=big(60),
    )(*operands)

    def to_analysis(x):
        return [lax.ppermute(x, "sec", [(i, sections - 1)]) for i in range(sections - 1)]

    terms = lax.all_to_all(parts, "dev", split_axis=0, concat_axis=0, tiled=True)
    total = jnp.sum(terms, axis=0)
    terms = to_analysis(total)
    wide, *terms = lax.optimization_barrier((wide, *terms))
    pieces = to_analysis(wide)

    def exchange(terms):
        total = jnp.broadcast_to(sum(terms[1:], terms[0])[None], parts.shape)
        return lax.all_to_all(total, "dev", split_axis=0, concat_axis=0, tiled=True)

    sums = lax.cond(analysis, exchange, lambda terms: jnp.zeros(parts.shape, f32), terms)
    sums = sums.reshape(columns * share, 8, LANES)

    scale = math.sqrt(columns * columns * CAP * depth)
    operands = (sums, scaled, gram)
    factor, inverse = pl.pallas_call(
        functools.partial(factor_kernel, scale, sections),
        out_shape=(jax.ShapeDtypeStruct((rank, rank), f32),) * 2,
        in_specs=vmem(*operands),
        out_specs=tuple(vmem(0, 0)),
        scratch_shapes=[pltpu.VMEM((rank, rank), f32)] * 2 + [pltpu.VMEM((2, 160, LANES), f32)],
        compiler_params=big(),
    )(*operands)
    operands = (inverse, scaled, sketch_in, *pieces)
    rows = 512

    def whole(x):
        return pl.BlockSpec(x.shape, lambda i: (0, 0))

    def strip(x):
        return pl.BlockSpec((rows, x.shape[1]), lambda i: (i, 0))

    basis = pl.pallas_call(
        functools.partial(basis_kernel, sections),
        out_shape=jax.ShapeDtypeStruct(sketch_in.shape, jnp.bfloat16),
        grid=(sketch_in.shape[0] // rows,),
        in_specs=[whole(inverse), whole(scaled), strip(sketch_in)] + [strip(x) for x in pieces],
        out_specs=strip(sketch_in),
        scratch_shapes=[pltpu.VMEM((2 * rank + 4 * snaps, rank), jnp.bfloat16)],
        compiler_params=big(60),
    )(*operands)
    return (basis[None], factor[None])


def solution(mesh):
    placed = (
        P("dev", None, "sec"),
        P("dev", None, "sec"),
        P("dev", None, "sec"),
        P("dev", None),
        P(),
        P("dev", None),
        P("dev", None),
    )
    return jax.shard_map(
        shards,
        mesh=mesh,
        in_specs=placed,
        out_specs=(P("sec", "dev", None), P("sec", None, None)),
        check_vma=False,
    )
```

profile of v0, /device:TPU:5, one launch (start us, length us, event | category | flops | bytes accessed | tf_op | source)
XLA Modules:
  0.0 176.8 jit_solution(17331548594402361643)
XLA Ops:
  0.7 46.4 %conditional.3 = (f32[512,512]{1,0:T(8,128)S(1)}) conditional(s32[]{:T(128)} %convert_element_type.13, () %tuple.31, bf16[2048,512]{1,0:T(8,128)(2,1)} %s_ref.1), branch_computations={%region_0.0_spmd, %region_1.0_spmd} | conditional | flops 1073971200 | bytes 9699340 | solution.py:543
  0.7 3.7 %fusion = f32[512,512]{1,0:T(8,128)S(1)} fusion(bf16[2048,512]{1,0:T(8,128)(2,1)} %param.1), kind=kOutput, calls=%fused_computation.3 | convolution fusion | flops 1073741824 | bytes 3145728 | tf_op jit(solution)/shard_map/cond/branch_1_fun/dot_general | solution.py:518
  4.4 24.7 %all_to_all.31 = f32[8,64,512]{2,1,0:T(8,128)S(1)} all-to-all(f32[8,64,512]{2,1,0:T(8,128)S(1)} %bitcast.10), channel_id=1, replica_groups=mesh['sec'=4,'dev'=8] {'dev'}, dimensions={0} | all-to-all | bytes 2097152 | tf_op jit(solution)/shard_map/cond/branch_1_fun/all_to_all | solution.py:522
  29.3 17.7 %all_to_all.32 = f32[8,64,512]{2,1,0:T(8,128)S(1)} all-to-all(f32[8,64,512]{2,1,0:T(8,128)S(1)} %broadcast_in_dim.5), channel_id=1, replica_groups=mesh['sec'=4,'dev'=8] {'dev'}, dimensions={0} | all-to-all | bytes 2097152 | tf_op jit(solution)/shard_map/cond/branch_1_fun/all_to_all | solution.py:524
  47.1 1.1 shard_map.98
  48.2 3.7 %all-to-all-start.4 = ((f32[8,104,128]{2,1,0:T(8,128)}), f32[8,104,128]{2,1,0:T(8,128)S(1)}, u32[]{:S(2)}, u32[]{:S(2)}) async-start(f32[8,104,128]{2,1,0:T(8,128)} %shard_map.98), calls=%async_computation.4 | async-start | bytes 851968 | tf_op jit(solution)/shard_map/all_to_all | solution.py:541
  52.0 9.2 %all-to-all-done.4.args_2_.args_5_ = f32[8,104,128]{2,1,0:T(8,128)S(1)} async-done(((f32[8,104,128]{2,1,0:T(8,128)}), f32[8,104,128]{2,1,0:T(8,128)S(1)}, u32[]{:S(2)}, u32[]{:S(2)}) %all-to-all-start.4) | async-done | bytes 426016 | tf_op jit(solution)/shard_map/all_to_all | solution.py:541
  61.9 0.7 collective-permute-start
  62.6 0.7 shard_map.99
  63.3 0.7 collective-permute-start.3
  64.0 0.7 collective-permute-start.2
  64.7 0.7 shard_map.100
  65.4 0.7 collective-permute-start.5
  66.1 0.7 collective-permute-start.4
  66.8 0.7 shard_map.101
  67.5 0.8 collective-permute-start.7
  69.0 1.3 shard_map.102
  71.0 10.1 %all_to_all.35.args_1_ = f32[8,8,8,128]{3,2,1,0:T(8,128)} all-to-all(f32[8,8,8,128]{3,2,1,0:T(8,128)S(1)} %get-tuple-element.51), channel_id=1, replica_groups=mesh['sec'=4,'dev'=8] {'dev'}, dimensions={0} | all-to-all | bytes 524288 | tf_op jit(solution)/shard_map/all_to_all | solution.py:579
  81.2 2.1 %shard_map.103 = (f32[8,5,8,128]{3,2,1,0:T(8,128)}, f32[2048,128]{1,0:T(8,128)}) custom-call(s32[8,2,9]{2,1,0:T(2,128)} %copy-done.2, f32[8,8,8,128]{3,2,1,0:T(8,128)} %all_to_all.35.args_1_, f32[8,8,8,128]{3,2,1,0:T(8,128)S(1)} %get-tuple-element.65.args_2_, bf16[2048,512]{1,0:T(8,128)(2,1)S(1)} %copy-done.8), custom_call_target="tpu_custom_call" | custom-call | tf_op jit(solution)/shard_map/pallas_call | solution.py:586
  83.3 9.7 %all_to_all.36 = f32[8,5,8,128]{3,2,1,0:T(8,128)S(1)} all-to-all(f32[8,5,8,128]{3,2,1,0:T(8,128)} %get-tuple-element.55), channel_id=1, replica_groups=mesh['sec'=4,'dev'=8] {'dev'}, dimensions={0} | all-to-all | bytes 327680 | tf_op jit(solution)/shard_map/all_to_all | solution.py:600
  93.0 1.3 collective-permute-start.10
  94.3 1.3 collective-permute-start.9
  95.6 1.3 collective-permute-start.8
  96.9 40.9 %collective-permute-done.10 = f32[5,8,128]{2,1,0:T(8,128)S(1)} collective-permute-done((f32[5,8,128]{2,1,0:T(8,128)S(1)}, f32[5,8,128]{2,1,0:T(8,128)S(1)}, u32[]{:S(2)}, u32[]{:S(2)}) %collective-permute-start.10) | collective-permute-done | bytes 20512 | tf_op jit(solution)/shard_map/ppermute | solution.py:598
  137.9 1.3 collective-permute-start.13
  139.2 1.3 collective-permute-start.12
  140.5 1.3 collective-permute-start.11
  141.8 8.9 %conditional.5 = (f32[40,8,128]{2,1,0:T(8,128)S(1)}) conditional(s32[]{:T(128)} %convert_element_type.13, () %tuple.30, (f32[5,8,128]{2,1,0:T(8,128)S(1)}, f32[5,8,128]{2,1,0:T(8,128)S(1)}, f32[5,8,128]{2,1,0:T(8,128)S(1)}) %tuple.34), branch_computations={%region_6.0_spmd, %region_7.0_spmd} | conditional | flops 10240 | bytes 593928 | solution.py:610
  141.8 8.8 %all_to_all.34 = f32[8,5,8,128]{3,2,1,0:T(8,128)S(1)} all-to-all(f32[8,5,8,128]{3,2,1,0:T(8,128)S(1)} %broadcast_in_dim.10), channel_id=1, replica_groups=mesh['sec'=4,'dev'=8] {'dev'}, dimensions={0} | all-to-all | bytes 327680 | tf_op jit(solution)/shard_map/cond/branch_1_fun/all_to_all | solution.py:608
  150.6 18.5 %shard_map.104 = (f32[512,512]{1,0:T(8,128)}, f32[512,512]{1,0:T(8,128)S(1)}) custom-call(f32[40,8,128]{2,1,0:T(8,128)S(1)} %get-tuple-element.66.refs_0_, f32[64,512]{1,0:T(8,128)S(1)} %broadcast_multiply_fusion.refs_1_.omega_ref, f32[512,512]{1,0:T(8,128)S(1)} %copy-done.10), custom_call_target="tpu_custom_call" | custom-call | tf_op jit(solution)/shard_map/pallas_call | solution.py:615
  169.1 1.0 copy-done.1
  170.1 6.7 %shard_map.105 = bf16[2048,512]{1,0:T(8,128)(2,1)} custom-call(f32[512,512]{1,0:T(8,128)} %copy-done.1, f32[64,512]{1,0:T(8,128)} %copy-done, bf16[2048,512]{1,0:T(8,128)(2,1)S(1)} %copy-done.8, f32[2048,128]{1,0:T(8,128)} %collective-permute-done.11.rest_0_, f32[2048,128]{1,0:T(8,128)} %collective-permute-done.12.rest_1_, ...), custom_call_target="tpu_custom_call" | custom-call | tf_op jit(solution)/shard_map/pallas_call | solution.py:632
  (49 shorter events, 1.8 us)
Async XLA Ops:
  0.6 46.4 %copy-start.3 = (f32[8,32,128]{2,1,0:T(8,128)S(1)}, f32[8,32,128]{2,1,0:T(8,128)}, u32[]{:S(2)}) copy-start(f32[8,32,128]{2,1,0:T(8,128)} %u_ref.1) | copy-start | bytes 393220
  0.6 46.4 %copy-start.4 = (f32[8,32,128]{2,1,0:T(8,128)S(1)}, f32[8,32,128]{2,1,0:T(8,128)}, u32[]{:S(2)}) copy-start(f32[8,32,128]{2,1,0:T(8,128)} %e_ref.1) | copy-start | bytes 393220
  0.7 46.4 %copy-start.5 = (f32[8,32,128]{2,1,0:T(8,128)S(1)}, f32[8,32,128]{2,1,0:T(8,128)}, u32[]{:S(2)}) copy-start(f32[8,32,128]{2,1,0:T(8,128)} %k_ref.1) | copy-start | bytes 393220
  0.7 46.4 %copy-start.6 = (s32[1,9]{1,0:T(1,128)S(1)}, s32[1,9]{1,0:T(1,128)}, u32[]{:S(2)}) copy-start(s32[1,9]{1,0:T(1,128)} %blocks_ref.1) | copy-start | bytes 112
  0.7 46.4 %copy-start.7 = (s32[1,9]{1,0:T(1,128)S(1)}, s32[1,9]{1,0:T(1,128)}, u32[]{:S(2)}) copy-start(s32[1,9]{1,0:T(1,128)} %owners_ref.1) | copy-start | bytes 112
  0.7 51.2 %copy-start.11 = (f32[64,512]{1,0:T(8,128)S(1)}, f32[64,512]{1,0:T(8,128)}, u32[]{:S(2)}) copy-start(f32[64,512]{1,0:T(8,128)} %param.18) | copy-start | bytes 393220
  0.7 51.2 %copy-start.12 = (f32[64]{0:T(128)S(1)}, f32[64]{0:T(128)}, u32[]{:S(2)}) copy-start(f32[64]{0:T(128)} %constant.21.clone) | copy-start | bytes 772
  47.1 15.5 %copy-start.9 = (f32[512,512]{1,0:T(8,128)}, f32[512,512]{1,0:T(8,128)S(1)}, u32[]{:S(2)}) copy-start(f32[512,512]{1,0:T(8,128)S(1)} %get-tuple-element.64.refs_2_) | copy-start | bytes 3145732
  48.2 13.0 %all-to-all-start.4 = ((f32[8,104,128]{2,1,0:T(8,128)}), f32[8,104,128]{2,1,0:T(8,128)S(1)}, u32[]{:S(2)}, u32[]{:S(2)}) async-start(f32[8,104,128]{2,1,0:T(8,128)} %shard_map.98), calls=%async_computation.4 | async-start | bytes 851968 | tf_op jit(solution)/shard_map/all_to_all | solution.py:541
  52.0 98.6 %copy-start = (f32[64,512]{1,0:T(8,128)}, f32[64,512]{1,0:T(8,128)S(1)}, u32[]{:S(2)}) copy-start(f32[64,512]{1,0:T(8,128)S(1)} %broadcast_multiply_fusion.refs_1_.omega_ref) | copy-start | bytes 393220
  61.2 1.4 collective-permute-start.1
  61.9 0.7 collective-permute-start
  62.6 6.5 %copy-start.2 = (s32[8,2,9]{2,1,0:T(2,128)}, s32[8,2,9]{2,1,0:T(2,128)S(1)}, u32[]{:S(2)}) copy-start(s32[8,2,9]{2,1,0:T(2,128)S(1)} %slice_convert_fusion.args_0_) | copy-start | bytes 1732
  63.3 1.4 collective-permute-start.3
  64.0 0.7 collective-permute-start.2
  65.4 1.4 collective-permute-start.5
  66.1 0.7 collective-permute-start.4
  67.5 13.7 %copy-start.8 = (bf16[2048,512]{1,0:T(8,128)(2,1)S(1)}, bf16[2048,512]{1,0:T(8,128)(2,1)}, u32[]{:S(2)}) copy-start(bf16[2048,512]{1,0:T(8,128)(2,1)} %s_ref.1) | copy-start | bytes 6291460
  67.5 1.5 collective-permute-start.7
  68.3 0.7 collective-permute-start.6
  81.2 69.5 %copy-start.10 = (f32[512,512]{1,0:T(8,128)S(1)}, f32[512,512]{1,0:T(8,128)}, u32[]{:S(2)}) copy-start(f32[512,512]{1,0:T(8,128)} %copy-done.9) | copy-start | bytes 3145732
  93.0 44.8 %collective-permute-start.10 = (f32[5,8,128]{2,1,0:T(8,128)S(1)}, f32[5,8,128]{2,1,0:T(8,128)S(1)}, u32[]{:S(2)}, u32[]{:S(2)}) collective-permute-start(f32[5,8,128]{2,1,0:T(8,128)S(1)} %reduce_sum.18), channel_id=1, source_target_pairs={{16,24},{17,25},{18,26},{19,27},{20,28},{21,29},{22,30},{23,31}} | collective-permute-start | bytes 61448 | tf_op jit(solution)/shard_map/ppermute | solution.py:598
  94.3 43.5 %collective-permute-start.9 = (f32[5,8,128]{2,1,0:T(8,128)S(1)}, f32[5,8,128]{2,1,0:T(8,128)S(1)}, u32[]{:S(2)}, u32[]{:S(2)}) collective-permute-start(f32[5,8,128]{2,1,0:T(8,128)S(1)} %reduce_sum.18), channel_id=1, source_target_pairs={{8,24},{9,25},{10,26},{11,27},{12,28},{13,29},{14,30},{15,31}} | collective-permute-start | bytes 61448 | tf_op jit(solution)/shard_map/ppermute | solution.py:598
  95.6 42.3 %collective-permute-start.8 = (f32[5,8,128]{2,1,0:T(8,128)S(1)}, f32[5,8,128]{2,1,0:T(8,128)S(1)}, u32[]{:S(2)}, u32[]{:S(2)}) collective-permute-start(f32[5,8,128]{2,1,0:T(8,128)S(1)} %reduce_sum.18), channel_id=1, source_target_pairs={{0,24},{1,25},{2,26},{3,27},{4,28},{5,29},{6,30},{7,31}} | collective-permute-start | bytes 61448 | tf_op jit(solution)/shard_map/ppermute | solution.py:598
  137.9 32.2 %collective-permute-start.13 = (f32[2048,128]{1,0:T(8,128)}, f32[2048,128]{1,0:T(8,128)}, u32[]{:S(2)}, u32[]{:S(2)}) collective-permute-start(f32[2048,128]{1,0:T(8,128)} %get-tuple-element.62), channel_id=1, source_target_pairs={{16,24},{17,25},{18,26},{19,27},{20,28},{21,29},{22,30},{23,31}} | collective-permute-start | bytes 3145736 | tf_op jit(solution)/shard_map/ppermute | solution.py:598
  139.2 30.9 %collective-permute-start.12 = (f32[2048,128]{1,0:T(8,128)}, f32[2048,128]{1,0:T(8,128)}, u32[]{:S(2)}, u32[]{:S(2)}) collective-permute-start(f32[2048,128]{1,0:T(8,128)} %get-tuple-element.62), channel_id=1, source_target_pairs={{8,24},{9,25},{10,26},{11,27},{12,28},{13,29},{14,30},{15,31}} | collective-permute-start | bytes 3145736 | tf_op jit(solution)/shard_map/ppermute | solution.py:598
  140.5 29.6 %collective-permute-start.11 = (f32[2048,128]{1,0:T(8,128)}, f32[2048,128]{1,0:T(8,128)}, u32[]{:S(2)}, u32[]{:S(2)}) collective-permute-start(f32[2048,128]{1,0:T(8,128)} %get-tuple-element.62), channel_id=1, source_target_pairs={{0,24},{1,25},{2,26},{3,27},{4,28},{5,29},{6,30},{7,31}} | collective-permute-start | bytes 3145736 | tf_op jit(solution)/shard_map/ppermute | solution.py:598
  169.1 1.0 copy-start.1
where the time goes:
time: 177 us
  blocking collectives  71.2 us (40%)
  waiting for transfers between devices  50.1 us (28%)
  Pallas kernels  31.7 us (18%)
  starting transfers between devices  17 us (10%)
  matrix products  3.66 us (2%)
    all_to_all x2, blocking collectives, whole_gram(): own = lax.all_to_all(own, 'dev', split_axis=0, concat_axis=0, tiled=True)  42.5 us
    ppermute x6, waiting for transfers between devices, to_analysis(): lax.ppermute(x, 'sec', [(i, sections - 1)])  41 us
    pallas_call x1, Pallas kernels, shards(): pl.pallas_call(functools.partial(factor_kernel, scale, sections), out_sha...  18.5 us
    all_to_all x1, blocking collectives, trade(): return lax.all_to_all(x, 'dev', split_axis=0, concat_axis=0, tiled=True)  10.1 us
    all_to_all x1, blocking collectives, shards(): lax.all_to_all(parts, 'dev', split_axis=0, concat_axis=0, tiled=True)  9.73 us
    all_to_all x1, waiting for transfers between devices, shards(): lax.all_to_all(outgoing, 'dev', split_axis=0, concat_axis=0, tiled=True)  9.16 us
    all_to_all x1, blocking collectives, exchange(): return lax.all_to_all(total, 'dev', split_axis=0, concat_axis=0, tiled=True)  8.81 us
    ppermute x6, starting transfers between devices, to_analysis(): lax.ppermute(x, 'sec', [(i, sections - 1)])  7.74 us
  transfers between devices with their start and end apart: 15, of which 2 were waited for; matrix products, arithmetic and copies ran while one was open for 0% of the time, Pallas kernels for 10%

commit v1 on v0

--- a/solution.py
+++ b/solution.py
@@ -621,7 +621,7 @@
         compiler_params=big(),
     )(*operands)
     operands = (inverse, scaled, sketch_in, *pieces)
-    rows = 512
+    rows = 1024
 
     def whole(x):
         return pl.BlockSpec(x.shape, lambda i: (0, 0))

time: 177 us -> 177 us (level)
  no operation moved by 1% of the time
where the time goes in v1:
time: 177 us; the launch traced here: 176 us
  blocking collectives  71.2 us (40%)
  waiting for transfers between devices  49.7 us (28%)
  Pallas kernels  31.2 us (18%)
  starting transfers between devices  17 us (10%)
  matrix products  3.66 us (2%)
    all_to_all x2, blocking collectives, whole_gram(): own = lax.all_to_all(own, 'dev', split_axis=0, concat_axis=0, tiled=True)  42.5 us
    ppermute x6, waiting for transfers between devices, to_analysis(): lax.ppermute(x, 'sec', [(i, sections - 1)])  40.5 us
    pallas_call x1, Pallas kernels, shards(): pl.pallas_call(functools.partial(factor_kernel, scale, sections), out_sha...  18.5 us
    all_to_all x1, blocking collectives, trade(): return lax.all_to_all(x, 'dev', split_axis=0, concat_axis=0, tiled=True)  10.1 us
    all_to_all x1, blocking collectives, shards(): lax.all_to_all(parts, 'dev', split_axis=0, concat_axis=0, tiled=True)  9.73 us
    all_to_all x1, waiting for transfers between devices, shards(): lax.all_to_all(outgoing, 'dev', split_axis=0, concat_axis=0, tiled=True)  9.16 us
    all_to_all x1, blocking collectives, exchange(): return lax.all_to_all(total, 'dev', split_axis=0, concat_axis=0, tiled=True)  8.81 us
    ppermute x6, starting transfers between devices, to_analysis(): lax.ppermute(x, 'sec', [(i, sections - 1)])  7.74 us
  transfers between devices with their start and end apart: 15, of which 2 were waited for; matrix products, arithmetic and copies ran while one was open for 0% of the time, Pallas kernels for 10%

profile of v1, /device:TPU:5, one launch (start us, length us, event | category | flops | bytes accessed | tf_op | source)
XLA Modules:
  0.0 175.9 jit_solution(6680830372344705308)
XLA Ops:
  0.7 46.4 %conditional.3 = (f32[512,512]{1,0:T(8,128)S(1)}) conditional(s32[]{:T(128)} %convert_element_type.13, () %tuple.31, bf16[2048,512]{1,0:T(8,128)(2,1)} %s_ref.1), branch_computations={%region_0.0_spmd, %region_1.0_spmd} | conditional | flops 1073971200 | bytes 9699340 | solution.py:543
  0.7 3.7 %fusion = f32[512,512]{1,0:T(8,128)S(1)} fusion(bf16[2048,512]{1,0:T(8,128)(2,1)} %param.1), kind=kOutput, calls=%fused_computation.3 | convolution fusion | flops 1073741824 | bytes 3145728 | tf_op jit(solution)/shard_map/cond/branch_1_fun/dot_general | solution.py:518
  4.4 24.7 %all_to_all.31 = f32[8,64,512]{2,1,0:T(8,128)S(1)} all-to-all(f32[8,64,512]{2,1,0:T(8,128)S(1)} %bitcast.10), channel_id=1, replica_groups=mesh['sec'=4,'dev'=8] {'dev'}, dimensions={0} | all-to-all | bytes 2097152 | tf_op jit(solution)/shard_map/cond/branch_1_fun/all_to_all | solution.py:522
  29.3 17.7 %all_to_all.32 = f32[8,64,512]{2,1,0:T(8,128)S(1)} all-to-all(f32[8,64,512]{2,1,0:T(8,128)S(1)} %broadcast_in_dim.5), channel_id=1, replica_groups=mesh['sec'=4,'dev'=8] {'dev'}, dimensions={0} | all-to-all | bytes 2097152 | tf_op jit(solution)/shard_map/cond/branch_1_fun/all_to_all | solution.py:524
  47.1 1.1 shard_map.98
  48.2 3.7 %all-to-all-start.4 = ((f32[8,104,128]{2,1,0:T(8,128)}), f32[8,104,128]{2,1,0:T(8,128)S(1)}, u32[]{:S(2)}, u32[]{:S(2)}) async-start(f32[8,104,128]{2,1,0:T(8,128)} %shard_map.98), calls=%async_computation.4 | async-start | bytes 851968 | tf_op jit(solution)/shard_map/all_to_all | solution.py:541
  52.0 9.2 %all-to-all-done.4.args_2_.args_5_ = f32[8,104,128]{2,1,0:T(8,128)S(1)} async-done(((f32[8,104,128]{2,1,0:T(8,128)}), f32[8,104,128]{2,1,0:T(8,128)S(1)}, u32[]{:S(2)}, u32[]{:S(2)}) %all-to-all-start.4) | async-done | bytes 426016 | tf_op jit(solution)/shard_map/all_to_all | solution.py:541
  61.9 0.7 collective-permute-start
  62.6 0.7 shard_map.99
  63.3 0.7 collective-permute-start.3
  64.0 0.7 collective-permute-start.2
  64.7 0.7 shard_map.100
  65.4 0.7 collective-permute-start.5
  66.1 0.7 collective-permute-start.4
  66.8 0.7 shard_map.101
  67.5 0.8 collective-permute-start.7
  69.0 1.3 shard_map.102
  71.0 10.1 %all_to_all.35.args_1_ = f32[8,8,8,128]{3,2,1,0:T(8,128)} all-to-all(f32[8,8,8,128]{3,2,1,0:T(8,128)S(1)} %get-tuple-element.51), channel_id=1, replica_groups=mesh['sec'=4,'dev'=8] {'dev'}, dimensions={0} | all-to-all | bytes 524288 | tf_op jit(solution)/shard_map/all_to_all | solution.py:579
  81.2 2.1 %shard_map.103 = (f32[8,5,8,128]{3,2,1,0:T(8,128)}, f32[2048,128]{1,0:T(8,128)}) custom-call(s32[8,2,9]{2,1,0:T(2,128)} %copy-done.2, f32[8,8,8,128]{3,2,1,0:T(8,128)} %all_to_all.35.args_1_, f32[8,8,8,128]{3,2,1,0:T(8,128)S(1)} %get-tuple-element.65.args_2_, bf16[2048,512]{1,0:T(8,128)(2,1)S(1)} %copy-done.8), custom_call_target="tpu_custom_call" | custom-call | tf_op jit(solution)/shard_map/pallas_call | solution.py:586
  83.3 9.7 %all_to_all.36 = f32[8,5,8,128]{3,2,1,0:T(8,128)S(1)} all-to-all(f32[8,5,8,128]{3,2,1,0:T(8,128)} %get-tuple-element.55), channel_id=1, replica_groups=mesh['sec'=4,'dev'=8] {'dev'}, dimensions={0} | all-to-all | bytes 327680 | tf_op jit(solution)/shard_map/all_to_all | solution.py:600
  93.0 1.3 collective-permute-start.10
  94.3 1.3 collective-permute-start.9
  95.6 1.3 collective-permute-start.8
  96.9 40.5 %collective-permute-done.10 = f32[5,8,128]{2,1,0:T(8,128)S(1)} collective-permute-done((f32[5,8,128]{2,1,0:T(8,128)S(1)}, f32[5,8,128]{2,1,0:T(8,128)S(1)}, u32[]{:S(2)}, u32[]{:S(2)}) %collective-permute-start.10) | collective-permute-done | bytes 20512 | tf_op jit(solution)/shard_map/ppermute | solution.py:598
  137.5 1.3 collective-permute-start.13
  138.7 1.3 collective-permute-start.12
  140.0 1.3 collective-permute-start.11
  141.3 8.9 %conditional.5 = (f32[40,8,128]{2,1,0:T(8,128)S(1)}) conditional(s32[]{:T(128)} %convert_element_type.13, () %tuple.30, (f32[5,8,128]{2,1,0:T(8,128)S(1)}, f32[5,8,128]{2,1,0:T(8,128)S(1)}, f32[5,8,128]{2,1,0:T(8,128)S(1)}) %tuple.34), branch_computations={%region_6.0_spmd, %region_7.0_spmd} | conditional | flops 10240 | bytes 593928 | solution.py:610
  141.4 8.8 %all_to_all.34 = f32[8,5,8,128]{3,2,1,0:T(8,128)S(1)} all-to-all(f32[8,5,8,128]{3,2,1,0:T(8,128)S(1)} %broadcast_in_dim.10), channel_id=1, replica_groups=mesh['sec'=4,'dev'=8] {'dev'}, dimensions={0} | all-to-all | bytes 327680 | tf_op jit(solution)/shard_map/cond/branch_1_fun/all_to_all | solution.py:608
  150.2 18.5 %shard_map.104 = (f32[512,512]{1,0:T(8,128)}, f32[512,512]{1,0:T(8,128)S(1)}) custom-call(f32[40,8,128]{2,1,0:T(8,128)S(1)} %get-tuple-element.66.refs_0_, f32[64,512]{1,0:T(8,128)S(1)} %broadcast_multiply_fusion.refs_1_.omega_ref, f32[512,512]{1,0:T(8,128)S(1)} %copy-done.10), custom_call_target="tpu_custom_call" | custom-call | tf_op jit(solution)/shard_map/pallas_call | solution.py:615
  168.7 1.0 copy-done.1
  169.7 6.2 %shard_map.105 = bf16[2048,512]{1,0:T(8,128)(2,1)} custom-call(f32[512,512]{1,0:T(8,128)} %copy-done.1, f32[64,512]{1,0:T(8,128)} %copy-done, bf16[2048,512]{1,0:T(8,128)(2,1)S(1)} %copy-done.8, f32[2048,128]{1,0:T(8,128)} %collective-permute-done.11.rest_0_, f32[2048,128]{1,0:T(8,128)} %collective-permute-done.12.rest_1_, ...), custom_call_target="tpu_custom_call" | custom-call | tf_op jit(solution)/shard_map/pallas_call | solution.py:632
  (49 shorter events, 1.8 us)
Async XLA Ops:
  0.6 46.4 %copy-start.3 = (f32[8,32,128]{2,1,0:T(8,128)S(1)}, f32[8,32,128]{2,1,0:T(8,128)}, u32[]{:S(2)}) copy-start(f32[8,32,128]{2,1,0:T(8,128)} %u_ref.1) | copy-start | bytes 393220
  0.6 46.4 %copy-start.4 = (f32[8,32,128]{2,1,0:T(8,128)S(1)}, f32[8,32,128]{2,1,0:T(8,128)}, u32[]{:S(2)}) copy-start(f32[8,32,128]{2,1,0:T(8,128)} %e_ref.1) | copy-start | bytes 393220
  0.7 46.4 %copy-start.5 = (f32[8,32,128]{2,1,0:T(8,128)S(1)}, f32[8,32,128]{2,1,0:T(8,128)}, u32[]{:S(2)}) copy-start(f32[8,32,128]{2,1,0:T(8,128)} %k_ref.1) | copy-start | bytes 393220
  0.7 46.4 %copy-start.6 = (s32[1,9]{1,0:T(1,128)S(1)}, s32[1,9]{1,0:T(1,128)}, u32[]{:S(2)}) copy-start(s32[1,9]{1,0:T(1,128)} %blocks_ref.1) | copy-start | bytes 112
  0.7 46.4 %copy-start.7 = (s32[1,9]{1,0:T(1,128)S(1)}, s32[1,9]{1,0:T(1,128)}, u32[]{:S(2)}) copy-start(s32[1,9]{1,0:T(1,128)} %owners_ref.1) | copy-start | bytes 112
  0.7 51.2 %copy-start.11 = (f32[64,512]{1,0:T(8,128)S(1)}, f32[64,512]{1,0:T(8,128)}, u32[]{:S(2)}) copy-start(f32[64,512]{1,0:T(8,128)} %param.18) | copy-start | bytes 393220
  0.7 51.2 %copy-start.12 = (f32[64]{0:T(128)S(1)}, f32[64]{0:T(128)}, u32[]{:S(2)}) copy-start(f32[64]{0:T(128)} %constant.21.clone) | copy-start | bytes 772
  47.1 15.5 %copy-start.9 = (f32[512,512]{1,0:T(8,128)}, f32[512,512]{1,0:T(8,128)S(1)}, u32[]{:S(2)}) copy-start(f32[512,512]{1,0:T(8,128)S(1)} %get-tuple-element.64.refs_2_) | copy-start | bytes 3145732
  48.2 13.0 %all-to-all-start.4 = ((f32[8,104,128]{2,1,0:T(8,128)}), f32[8,104,128]{2,1,0:T(8,128)S(1)}, u32[]{:S(2)}, u32[]{:S(2)}) async-start(f32[8,104,128]{2,1,0:T(8,128)} %shard_map.98), calls=%async_computation.4 | async-start | bytes 851968 | tf_op jit(solution)/shard_map/all_to_all | solution.py:541
  52.0 98.2 %copy-start = (f32[64,512]{1,0:T(8,128)}, f32[64,512]{1,0:T(8,128)S(1)}, u32[]{:S(2)}) copy-start(f32[64,512]{1,0:T(8,128)S(1)} %broadcast_multiply_fusion.refs_1_.omega_ref) | copy-start | bytes 393220
  61.2 1.4 collective-permute-start.1
  61.9 0.7 collective-permute-start
  62.6 6.5 %copy-start.2 = (s32[8,2,9]{2,1,0:T(2,128)}, s32[8,2,9]{2,1,0:T(2,128)S(1)}, u32[]{:S(2)}) copy-start(s32[8,2,9]{2,1,0:T(2,128)S(1)} %slice_convert_fusion.args_0_) | copy-start | bytes 1732
  63.3 1.4 collective-permute-start.3
  64.0 0.7 collective-permute-start.2
  65.4 1.4 collective-permute-start.5
  66.1 0.7 collective-permute-start.4
  67.5 13.7 %copy-start.8 = (bf16[2048,512]{1,0:T(8,128)(2,1)S(1)}, bf16[2048,512]{1,0:T(8,128)(2,1)}, u32[]{:S(2)}) copy-start(bf16[2048,512]{1,0:T(8,128)(2,1)} %s_ref.1) | copy-start | bytes 6291460
  67.5 1.5 collective-permute-start.7
  68.3 0.7 collective-permute-start.6
  81.2 69.0 %copy-start.10 = (f32[512,512]{1,0:T(8,128)S(1)}, f32[512,512]{1,0:T(8,128)}, u32[]{:S(2)}) copy-start(f32[512,512]{1,0:T(8,128)} %copy-done.9) | copy-start | bytes 3145732
  93.0 44.4 %collective-permute-start.10 = (f32[5,8,128]{2,1,0:T(8,128)S(1)}, f32[5,8,128]{2,1,0:T(8,128)S(1)}, u32[]{:S(2)}, u32[]{:S(2)}) collective-permute-start(f32[5,8,128]{2,1,0:T(8,128)S(1)} %reduce_sum.18), channel_id=1, source_target_pairs={{16,24},{17,25},{18,26},{19,27},{20,28},{21,29},{22,30},{23,31}} | collective-permute-start | bytes 61448 | tf_op jit(solution)/shard_map/ppermute | solution.py:598
  94.3 43.1 %collective-permute-start.9 = (f32[5,8,128]{2,1,0:T(8,128)S(1)}, f32[5,8,128]{2,1,0:T(8,128)S(1)}, u32[]{:S(2)}, u32[]{:S(2)}) collective-permute-start(f32[5,8,128]{2,1,0:T(8,128)S(1)} %reduce_sum.18), channel_id=1, source_target_pairs={{8,24},{9,25},{10,26},{11,27},{12,28},{13,29},{14,30},{15,31}} | collective-permute-start | bytes 61448 | tf_op jit(solution)/shard_map/ppermute | solution.py:598
  95.6 41.8 %collective-permute-start.8 = (f32[5,8,128]{2,1,0:T(8,128)S(1)}, f32[5,8,128]{2,1,0:T(8,128)S(1)}, u32[]{:S(2)}, u32[]{:S(2)}) collective-permute-start(f32[5,8,128]{2,1,0:T(8,128)S(1)} %reduce_sum.18), channel_id=1, source_target_pairs={{0,24},{1,25},{2,26},{3,27},{4,28},{5,29},{6,30},{7,31}} | collective-permute-start | bytes 61448 | tf_op jit(solution)/shard_map/ppermute | solution.py:598
  137.5 32.2 %collective-permute-start.13 = (f32[2048,128]{1,0:T(8,128)}, f32[2048,128]{1,0:T(8,128)}, u32[]{:S(2)}, u32[]{:S(2)}) collective-permute-start(f32[2048,128]{1,0:T(8,128)} %get-tuple-element.62), channel_id=1, source_target_pairs={{16,24},{17,25},{18,26},{19,27},{20,28},{21,29},{22,30},{23,31}} | collective-permute-start | bytes 3145736 | tf_op jit(solution)/shard_map/ppermute | solution.py:598
  138.7 30.9 %collective-permute-start.12 = (f32[2048,128]{1,0:T(8,128)}, f32[2048,128]{1,0:T(8,128)}, u32[]{:S(2)}, u32[]{:S(2)}) collective-permute-start(f32[2048,128]{1,0:T(8,128)} %get-tuple-element.62), channel_id=1, source_target_pairs={{8,24},{9,25},{10,26},{11,27},{12,28},{13,29},{14,30},{15,31}} | collective-permute-start | bytes 3145736 | tf_op jit(solution)/shard_map/ppermute | solution.py:598
  140.0 29.6 %collective-permute-start.11 = (f32[2048,128]{1,0:T(8,128)}, f32[2048,128]{1,0:T(8,128)}, u32[]{:S(2)}, u32[]{:S(2)}) collective-permute-start(f32[2048,128]{1,0:T(8,128)} %get-tuple-element.62), channel_id=1, source_target_pairs={{0,24},{1,25},{2,26},{3,27},{4,28},{5,29},{6,30},{7,31}} | collective-permute-start | bytes 3145736 | tf_op jit(solution)/shard_map/ppermute | solution.py:598
  168.7 1.0 copy-start.1
